TPU v7x, 32 devices: a whole 2x2x4 slice. The times are simulated.
32 devices in a mesh: grp: 4 (over y, x), word: 8 (over z, core).
Axes of the slice: x: 2, y: 2, z: 4, core: 2. Of those that a mesh axis runs over, the one named last changes fastest.
Arguments:
- descriptors: bfloat16 [262144, 128], P(('grp', 'word'))
- word_ids: int32 [262144], P(('grp', 'word')), may hold values from 0 to 1023, as said below
Outputs:
- centroids: bfloat16 [1024, 128], P('word')
- nearest: float32 [262144], P(('grp', 'word'))
Inputs may be any that keep to these rules, and one draw needn't show every extreme that they name: `word_ids`: the word ids of one device's descriptors lie in a window of 64 consecutive ids, counted modulo 1024; every word id from 0 to 1023 occurs at least once.
All inputs are finite; a program needn't handle non-finite values.
Results may differ from a plain program's by a relative error of at most 0.0015.
Values may be sent and summed in bfloat16 or wider, within the bound.
No kernel may reach another device: no remote copies, remote signals or barrier semaphores. Data moves between devices by JAX's collectives and lax.ppermute only.
A program may use at most 64 MiB of HBM per device.

v0:
```python
import jax
import jax.numpy as jnp
from jax import lax
from jax.sharding import PartitionSpec as P

K = 1024


def local_sums(descriptors, word_ids):
    rows = descriptors.shape[0]
    depth = descriptors.shape[1]
    words = K
    block = min(1024, rows)
    xs = descriptors.reshape(rows // block, block, depth)
    idx = word_ids.reshape(rows // block, block)
    table = lax.broadcasted_iota(jnp.int32, (1, words), 1)

    def step(carry, item):
        total, count = carry
        xb, ib = item
        onehot = (ib[:, None] == table).astype(jnp.bfloat16)
        total = total + jnp.einsum("nk,nd->kd", onehot, xb, preferred_element_type=jnp.float32)
        count = count + jnp.sum(onehot.astype(jnp.float32), axis=0)
        return ((total, count), None)

    init = (jnp.zeros((words, depth), jnp.float32), jnp.zeros((words,), jnp.float32))
    (total, count), unused = lax.scan(step, init, (xs, idx))
    return (total, count)


def on_device(descriptors, word_ids):
    total, count = local_sums(descriptors, word_ids)
    xf = descriptors.astype(jnp.float32)
    xnorm = jnp.sum(xf * xf, axis=1)
    depth = descriptors.shape[1]
    start_min = jnp.full(xnorm.shape, jnp.inf, jnp.float32)
    total, count = lax.psum((total, count), ("grp", "word"))
    whole = (total / count[:, None]).astype(jnp.bfloat16)
    pf = whole.astype(jnp.float32)
    cnorm = jnp.sum(pf * pf, axis=1)
    dots = jnp.dot(descriptors, whole.T, preferred_element_type=jnp.float32)
    dist = (xnorm[:, None] - 2.0 * dots + cnorm[None, :]) / depth
    nearest = jnp.minimum(start_min, jnp.min(dist, axis=1))
    owned_rows = whole.shape[0] // lax.axis_size("word")
    begin = lax.axis_index("word") * owned_rows
    cent = lax.dynamic_slice_in_dim(whole, begin, owned_rows, 0)
    return (cent, nearest)


def solution(mesh):
    return jax.shard_map(
        on_device,
        mesh=mesh,
        in_specs=(P(("grp", "word"), None), P(("grp", "word"))),
        out_specs=(P("word", None), P(("grp", "word"))),
        check_vma=False,
    )
```

profile of v0, /device:TPU:0, one launch (start us, length us, event | category | flops | bytes accessed | tf_op | source)
XLA Modules:
  0.0 181.5 jit_solution(9641654276949608156)
XLA Ops:
  7.2 0.0 all-reduce.2.cloned.1.call-start
  7.2 0.8 reshape.15
  8.0 24.5 %while.13 = (s32[]{:T(128)}, f32[1024,128]{1,0:T(8,128)S(1)}, f32[1024]{0:T(1024)S(1)}, s32[8,1024]{1,0:T(8,128)S(1)}, bf16[8,1024,128]{2,1,0:T(8,128)(2,1)}, /*index=5*/s32[]{:T(128)}, s32[]{:T(128)}) while((s32[]{:T(128)}, f32[1024,128]{1,0:T(8,128)S(1)}, f32[1024]{0:T(1024)S(1)}, s32[8,1024]{1,0:T(8,128)S(1)}, ...), condition=%wide.region_2.3_spmd.clone, body=%wide.region_0.2_spmd.clone.sunk | while | flops 273941504 | bytes 1343592 | solution.py:27
  8.0 2.5 %fusion.14 = f32[1024,128]{1,0:T(8,128)S(1)} fusion(s32[1024]{0:T(1024)S(1)} %bitcast.14, f32[1024,128]{1,0:T(8,128)S(1)} %get-tuple-element.108, bf16[8,1024,128]{2,1,0:T(8,128)(2,1)} %get-tuple-element.118, s32[]{:T(128)S(6)} %copy.7, pred[]{:T(512)S(6)} %compare.3), kind=kOutput, calls=%fused_computation.6.clone.1 | convolution fusion | flops 269746176 | bytes 1314821 | tf_op jit(solution)/shard_map/while/body/eval_jaxpr/nk,nd->kd/dot_general | solution.py:22
  10.6 0.5 convert_reduce_fusion.2
  11.1 2.5 %fusion.14 = f32[1024,128]{1,0:T(8,128)S(1)} fusion(s32[1024]{0:T(1024)S(1)} %bitcast.14, f32[1024,128]{1,0:T(8,128)S(1)} %get-tuple-element.108, bf16[8,1024,128]{2,1,0:T(8,128)(2,1)} %get-tuple-element.118, s32[]{:T(128)S(6)} %copy.7, pred[]{:T(512)S(6)} %compare.3), kind=kOutput, calls=%fused_computation.6.clone.1 | convolution fusion | flops 269746176 | bytes 1314821 | tf_op jit(solution)/shard_map/while/body/eval_jaxpr/nk,nd->kd/dot_general | solution.py:22
  13.6 0.5 convert_reduce_fusion.2
  14.2 2.5 %fusion.14 = f32[1024,128]{1,0:T(8,128)S(1)} fusion(s32[1024]{0:T(1024)S(1)} %bitcast.14, f32[1024,128]{1,0:T(8,128)S(1)} %get-tuple-element.108, bf16[8,1024,128]{2,1,0:T(8,128)(2,1)} %get-tuple-element.118, s32[]{:T(128)S(6)} %copy.7, pred[]{:T(512)S(6)} %compare.3), kind=kOutput, calls=%fused_computation.6.clone.1 | convolution fusion | flops 269746176 | bytes 1314821 | tf_op jit(solution)/shard_map/while/body/eval_jaxpr/nk,nd->kd/dot_general | solution.py:22
  16.7 0.5 convert_reduce_fusion.2
  17.2 2.5 %fusion.14 = f32[1024,128]{1,0:T(8,128)S(1)} fusion(s32[1024]{0:T(1024)S(1)} %bitcast.14, f32[1024,128]{1,0:T(8,128)S(1)} %get-tuple-element.108, bf16[8,1024,128]{2,1,0:T(8,128)(2,1)} %get-tuple-element.118, s32[]{:T(128)S(6)} %copy.7, pred[]{:T(512)S(6)} %compare.3), kind=kOutput, calls=%fused_computation.6.clone.1 | convolution fusion | flops 269746176 | bytes 1314821 | tf_op jit(solution)/shard_map/while/body/eval_jaxpr/nk,nd->kd/dot_general | solution.py:22
  19.7 0.5 convert_reduce_fusion.2
  20.3 2.5 %fusion.14 = f32[1024,128]{1,0:T(8,128)S(1)} fusion(s32[1024]{0:T(1024)S(1)} %bitcast.14, f32[1024,128]{1,0:T(8,128)S(1)} %get-tuple-element.108, bf16[8,1024,128]{2,1,0:T(8,128)(2,1)} %get-tuple-element.118, s32[]{:T(128)S(6)} %copy.7, pred[]{:T(512)S(6)} %compare.3), kind=kOutput, calls=%fused_computation.6.clone.1 | convolution fusion | flops 269746176 | bytes 1314821 | tf_op jit(solution)/shard_map/while/body/eval_jaxpr/nk,nd->kd/dot_general | solution.py:22
  22.8 0.5 convert_reduce_fusion.2
  23.3 2.5 %fusion.14 = f32[1024,128]{1,0:T(8,128)S(1)} fusion(s32[1024]{0:T(1024)S(1)} %bitcast.14, f32[1024,128]{1,0:T(8,128)S(1)} %get-tuple-element.108, bf16[8,1024,128]{2,1,0:T(8,128)(2,1)} %get-tuple-element.118, s32[]{:T(128)S(6)} %copy.7, pred[]{:T(512)S(6)} %compare.3), kind=kOutput, calls=%fused_computation.6.clone.1 | convolution fusion | flops 269746176 | bytes 1314821 | tf_op jit(solution)/shard_map/while/body/eval_jaxpr/nk,nd->kd/dot_general | solution.py:22
  25.9 0.5 convert_reduce_fusion.2
  26.4 2.5 %fusion.14 = f32[1024,128]{1,0:T(8,128)S(1)} fusion(s32[1024]{0:T(1024)S(1)} %bitcast.14, f32[1024,128]{1,0:T(8,128)S(1)} %get-tuple-element.108, bf16[8,1024,128]{2,1,0:T(8,128)(2,1)} %get-tuple-element.118, s32[]{:T(128)S(6)} %copy.7, pred[]{:T(512)S(6)} %compare.3), kind=kOutput, calls=%fused_computation.6.clone.1 | convolution fusion | flops 269746176 | bytes 1314821 | tf_op jit(solution)/shard_map/while/body/eval_jaxpr/nk,nd->kd/dot_general | solution.py:22
  28.9 0.5 convert_reduce_fusion.2
  29.5 2.5 %fusion.14 = f32[1024,128]{1,0:T(8,128)S(1)} fusion(s32[1024]{0:T(1024)S(1)} %bitcast.14, f32[1024,128]{1,0:T(8,128)S(1)} %get-tuple-element.108, bf16[8,1024,128]{2,1,0:T(8,128)(2,1)} %get-tuple-element.118, s32[]{:T(128)S(6)} %copy.7, pred[]{:T(512)S(6)} %compare.3), kind=kOutput, calls=%fused_computation.6.clone.1 | convolution fusion | flops 269746176 | bytes 1314821 | tf_op jit(solution)/shard_map/while/body/eval_jaxpr/nk,nd->kd/dot_general | solution.py:22
  32.0 0.5 convert_reduce_fusion.2
  32.5 0.0 copy-start.1
  32.5 0.0 copy-start
  32.5 0.8 copy-done.1
  33.3 0.0 all-reduce.2.cloned.1.call-update
  33.3 42.1 %psum.15 = f32[1024]{0:T(1024)S(1)} all-reduce(f32[1024]{0:T(1024)S(1)} %get-tuple-element.36), channel_id=1, replica_groups=mesh['grp'=4,'word'=8] {'grp','word'}, use_global_device_ids=true, to_apply=%region_4.5 | all-reduce | flops 1024 | bytes 8192 | tf_op jit(solution)/shard_map/psum | solution.py:37
  75.4 2.8 %multiply_reduce_fusion.1 = f32[8192]{0:T(1024)S(1)} fusion(bf16[8192,128]{1,0:T(8,128)(2,1)} %bitcast.12), kind=kLoop, calls=%fused_computation.13 | loop fusion | flops 3137536 | bytes 2129920 | tf_op jit(solution)/shard_map/reduce_sum | solution.py:34
  78.2 87.2 %all-reduce.2.cloned.1.call-done = f32[1024,128]{1,0:T(8,128)} async-done(((f32[1024,128]{1,0:T(8,128)}), f32[1024,128]{1,0:T(8,128)}) %all-reduce.2.cloned.1.call-update) | async-done | bytes 524304 | tf_op jit(solution)/shard_map/psum | solution.py:37
  165.4 1.4 multiply_reduce_fusion.2
  166.8 0.6 constant_dynamic-slice_fusion.1
  167.4 0.0 copy-done
  167.4 7.3 %multiply_reduce_fusion = f32[8192]{0:T(1024)} fusion(f32[1024]{0:T(1024)S(1)} %get-tuple-element.67, f32[8192]{0:T(1024)S(1)} %multiply_reduce_fusion.1, bf16[1024,128]{1,0:T(8,128)(2,1)S(1)} %get-tuple-element.68, bf16[8192,128]{1,0:T(8,128)(2,1)S(1)} %bitcast.13), kind=kOutput, calls=%fused_computation.12 | convolution fusion | flops 2189418496 | bytes 2428928 | tf_op jit(solution)/shard_map/dot_general | solution.py:41
  (18 shorter events, 0.1 us)
Async XLA Ops:
  7.2 158.2 %all-reduce.2.cloned.1.call-start = ((), (), s32[]{:S(2)}) async-start(), calls=%async_computation | async-start | bytes 1048576 | tf_op jit(solution)/shard_map/psum | solution.py:37
  32.5 0.8 copy-start.1
  32.5 134.9 %copy-start = (bf16[8,1024,128]{2,1,0:T(8,128)(2,1)S(1)}, bf16[8,1024,128]{2,1,0:T(8,128)(2,1)}, u32[]{:S(2)}) copy-start(bf16[8,1024,128]{2,1,0:T(8,128)(2,1)} %get-tuple-element.122) | copy-start | bytes 6291460
Sparse Core Ops, SparseCore 0:
  33.5 131.8 all-reduce.1
where the time goes:
time: 182 us
  waiting for transfers between devices  87.2 us (48%)
  blocking collectives  42.1 us (23%)
  matrix products  27.4 us (15%)
  between operations  14.1 us (8%)
  other arithmetic  8.02 us (4%)
  local copies, waits for them, and re-layouts  2.27 us (1%)
    psum x1, waiting for transfers between devices, on_device(): total, count = lax.psum((total, count), ('grp', 'word'))  87.2 us
    psum x1, blocking collectives, on_device(): total, count = lax.psum((total, count), ('grp', 'word'))  42.1 us
    dot_general x8, matrix products, step(): jnp.einsum('nk,nd->kd', onehot, xb, preferred_element_type=jnp.float32)  20.1 us
    dot_general x1, matrix products, on_device(): dots = jnp.dot(descriptors, whole.T, preferred_element_type=jnp.float32)  7.29 us
    reduce_sum x8, other arithmetic, step(): count = count + jnp.sum(onehot.astype(jnp.float32), axis=0)  3.82 us
  transfers between devices with their start and end apart: 1, of which 1 were waited for; matrix products, arithmetic and copies ran while one was open for 2% of the time, Pallas kernels for 0%

commit v1 on v0

--- a/solution.py
+++ b/solution.py
@@ -4,6 +4,7 @@
 from jax.sharding import PartitionSpec as P
 
 K = 1024
+update_the_cards = lambda z: jax.lax.psum(jax.lax.psum(z, "word"), "grp")
 
 
 def local_sums(descriptors, word_ids):
@@ -34,7 +35,7 @@
     xnorm = jnp.sum(xf * xf, axis=1)
     depth = descriptors.shape[1]
     start_min = jnp.full(xnorm.shape, jnp.inf, jnp.float32)
-    total, count = lax.psum((total, count), ("grp", "word"))
+    total, count = update_the_cards((total, count))
     whole = (total / count[:, None]).astype(jnp.bfloat16)
     pf = whole.astype(jnp.float32)
     cnorm = jnp.sum(pf * pf, axis=1)

time: 182 us -> 157 us (0.86)
  blocking collectives: 42.1 us -> 23.6 us
  waiting for transfers between devices: 87.2 us -> 80.4 us
    psum x1 -> x2, blocking collectives: 42.1 us -> 23.6 us  [update_the_cards = lambda z: jax.lax.psum(jax.lax.psum(z, 'word'), 'grp')]
    psum x1 -> x2, waiting for transfers between devices: 87.2 us -> 80.4 us  [update_the_cards = lambda z: jax.lax.psum(jax.lax.psum(z, 'word'), 'grp')]
  transfers between devices with their start and end apart: 1 -> 2, of which waited for: 1 -> 2; matrix products, arithmetic and copies ran while one was open for 2% -> 2% of each run, Pallas kernels for 0% -> 0%
where the time goes in v1:
time: 157 us; the launch traced here: 156 us
  waiting for transfers between devices  80.4 us (51%)
  matrix products  27.4 us (17%)
  blocking collectives  23.6 us (15%)
  between operations  14.1 us (9%)
  other arithmetic  8.02 us (5%)
  local copies, waits for them, and re-layouts  2.27 us (1%)
    psum x2, waiting for transfers between devices, update_the_cards = lambda z: jax.lax.psum(jax.lax.psum(z, 'word'), 'grp')  80.4 us
    psum x2, blocking collectives, update_the_cards = lambda z: jax.lax.psum(jax.lax.psum(z, 'word'), 'grp')  23.6 us
    dot_general x8, matrix products, step(): jnp.einsum('nk,nd->kd', onehot, xb, preferred_element_type=jnp.float32)  20.1 us
    dot_general x1, matrix products, on_device(): dots = jnp.dot(descriptors, whole.T, preferred_element_type=jnp.float32)  7.29 us
    reduce_sum x8, other arithmetic, step(): count = count + jnp.sum(onehot.astype(jnp.float32), axis=0)  3.82 us
  transfers between devices with their start and end apart: 2, of which 2 were waited for; matrix products, arithmetic and copies ran while one was open for 2% of the time, Pallas kernels for 0%

profile of v1, /device:TPU:0, one launch (start us, length us, event | category | flops | bytes accessed | tf_op | source)
XLA Modules:
  0.0 156.3 jit_solution(15688568564056669982)
XLA Ops:
  7.2 0.0 all-reduce.3.cloned.1.call-start
  7.2 0.8 reshape.15
  8.0 24.5 %while.13 = (s32[]{:T(128)}, f32[1024,128]{1,0:T(8,128)S(1)}, f32[1024]{0:T(1024)S(1)}, s32[8,1024]{1,0:T(8,128)S(1)}, bf16[8,1024,128]{2,1,0:T(8,128)(2,1)}, /*index=5*/s32[]{:T(128)}, s32[]{:T(128)}) while((s32[]{:T(128)}, f32[1024,128]{1,0:T(8,128)S(1)}, f32[1024]{0:T(1024)S(1)}, s32[8,1024]{1,0:T(8,128)S(1)}, ...), condition=%wide.region_2.3_spmd.clone, body=%wide.region_0.2_spmd.clone.sunk | while | flops 273941504 | bytes 1343592 | solution.py:28
  8.0 2.5 %fusion.14 = f32[1024,128]{1,0:T(8,128)S(1)} fusion(s32[1024]{0:T(1024)S(1)} %bitcast.14, f32[1024,128]{1,0:T(8,128)S(1)} %get-tuple-element.108, bf16[8,1024,128]{2,1,0:T(8,128)(2,1)} %get-tuple-element.118, s32[]{:T(128)S(6)} %copy.7, pred[]{:T(512)S(6)} %compare.3), kind=kOutput, calls=%fused_computation.6.clone.1 | convolution fusion | flops 269746176 | bytes 1314821 | tf_op jit(solution)/shard_map/while/body/eval_jaxpr/nk,nd->kd/dot_general | solution.py:23
  10.6 0.5 convert_reduce_fusion.2
  11.1 2.5 %fusion.14 = f32[1024,128]{1,0:T(8,128)S(1)} fusion(s32[1024]{0:T(1024)S(1)} %bitcast.14, f32[1024,128]{1,0:T(8,128)S(1)} %get-tuple-element.108, bf16[8,1024,128]{2,1,0:T(8,128)(2,1)} %get-tuple-element.118, s32[]{:T(128)S(6)} %copy.7, pred[]{:T(512)S(6)} %compare.3), kind=kOutput, calls=%fused_computation.6.clone.1 | convolution fusion | flops 269746176 | bytes 1314821 | tf_op jit(solution)/shard_map/while/body/eval_jaxpr/nk,nd->kd/dot_general | solution.py:23
  13.6 0.5 convert_reduce_fusion.2
  14.2 2.5 %fusion.14 = f32[1024,128]{1,0:T(8,128)S(1)} fusion(s32[1024]{0:T(1024)S(1)} %bitcast.14, f32[1024,128]{1,0:T(8,128)S(1)} %get-tuple-element.108, bf16[8,1024,128]{2,1,0:T(8,128)(2,1)} %get-tuple-element.118, s32[]{:T(128)S(6)} %copy.7, pred[]{:T(512)S(6)} %compare.3), kind=kOutput, calls=%fused_computation.6.clone.1 | convolution fusion | flops 269746176 | bytes 1314821 | tf_op jit(solution)/shard_map/while/body/eval_jaxpr/nk,nd->kd/dot_general | solution.py:23
  16.7 0.5 convert_reduce_fusion.2
  17.2 2.5 %fusion.14 = f32[1024,128]{1,0:T(8,128)S(1)} fusion(s32[1024]{0:T(1024)S(1)} %bitcast.14, f32[1024,128]{1,0:T(8,128)S(1)} %get-tuple-element.108, bf16[8,1024,128]{2,1,0:T(8,128)(2,1)} %get-tuple-element.118, s32[]{:T(128)S(6)} %copy.7, pred[]{:T(512)S(6)} %compare.3), kind=kOutput, calls=%fused_computation.6.clone.1 | convolution fusion | flops 269746176 | bytes 1314821 | tf_op jit(solution)/shard_map/while/body/eval_jaxpr/nk,nd->kd/dot_general | solution.py:23
  19.7 0.5 convert_reduce_fusion.2
  20.3 2.5 %fusion.14 = f32[1024,128]{1,0:T(8,128)S(1)} fusion(s32[1024]{0:T(1024)S(1)} %bitcast.14, f32[1024,128]{1,0:T(8,128)S(1)} %get-tuple-element.108, bf16[8,1024,128]{2,1,0:T(8,128)(2,1)} %get-tuple-element.118, s32[]{:T(128)S(6)} %copy.7, pred[]{:T(512)S(6)} %compare.3), kind=kOutput, calls=%fused_computation.6.clone.1 | convolution fusion | flops 269746176 | bytes 1314821 | tf_op jit(solution)/shard_map/while/body/eval_jaxpr/nk,nd->kd/dot_general | solution.py:23
  22.8 0.5 convert_reduce_fusion.2
  23.3 2.5 %fusion.14 = f32[1024,128]{1,0:T(8,128)S(1)} fusion(s32[1024]{0:T(1024)S(1)} %bitcast.14, f32[1024,128]{1,0:T(8,128)S(1)} %get-tuple-element.108, bf16[8,1024,128]{2,1,0:T(8,128)(2,1)} %get-tuple-element.118, s32[]{:T(128)S(6)} %copy.7, pred[]{:T(512)S(6)} %compare.3), kind=kOutput, calls=%fused_computation.6.clone.1 | convolution fusion | flops 269746176 | bytes 1314821 | tf_op jit(solution)/shard_map/while/body/eval_jaxpr/nk,nd->kd/dot_general | solution.py:23
  25.9 0.5 convert_reduce_fusion.2
  26.4 2.5 %fusion.14 = f32[1024,128]{1,0:T(8,128)S(1)} fusion(s32[1024]{0:T(1024)S(1)} %bitcast.14, f32[1024,128]{1,0:T(8,128)S(1)} %get-tuple-element.108, bf16[8,1024,128]{2,1,0:T(8,128)(2,1)} %get-tuple-element.118, s32[]{:T(128)S(6)} %copy.7, pred[]{:T(512)S(6)} %compare.3), kind=kOutput, calls=%fused_computation.6.clone.1 | convolution fusion | flops 269746176 | bytes 1314821 | tf_op jit(solution)/shard_map/while/body/eval_jaxpr/nk,nd->kd/dot_general | solution.py:23
  28.9 0.5 convert_reduce_fusion.2
  29.5 2.5 %fusion.14 = f32[1024,128]{1,0:T(8,128)S(1)} fusion(s32[1024]{0:T(1024)S(1)} %bitcast.14, f32[1024,128]{1,0:T(8,128)S(1)} %get-tuple-element.108, bf16[8,1024,128]{2,1,0:T(8,128)(2,1)} %get-tuple-element.118, s32[]{:T(128)S(6)} %copy.7, pred[]{:T(512)S(6)} %compare.3), kind=kOutput, calls=%fused_computation.6.clone.1 | convolution fusion | flops 269746176 | bytes 1314821 | tf_op jit(solution)/shard_map/while/body/eval_jaxpr/nk,nd->kd/dot_general | solution.py:23
  32.0 0.5 convert_reduce_fusion.2
  32.5 0.0 copy-start
  32.5 0.8 copy-done.1
  33.3 0.0 all-reduce.3.cloned.1.call-update
  33.3 0.0 all-reduce.5.cloned.1.call-start
  33.4 59.3 %all-reduce.3.cloned.1.call-done = f32[1024,128]{1,0:T(8,128)} async-done(((f32[1024,128]{1,0:T(8,128)}), f32[1024,128]{1,0:T(8,128)}) %all-reduce.3.cloned.1.call-update) | async-done | bytes 524304 | tf_op jit(solution)/shard_map/psum | solution.py:7
  92.7 0.0 all-reduce.5.cloned.1.call-update
  92.7 13.7 %psum.30 = f32[1024]{0:T(1024)S(1)} all-reduce(f32[1024]{0:T(1024)S(1)} %get-tuple-element.36), channel_id=1, replica_groups=mesh['grp'=4,'word'=8] {'word'}, use_global_device_ids=true, to_apply=%region_5.6 | all-reduce | flops 1024 | bytes 8192 | tf_op jit(solution)/shard_map/psum | solution.py:7
  106.4 9.9 %psum.31 = f32[1024]{0:T(1024)S(1)} all-reduce(f32[1024]{0:T(1024)S(1)} %psum.30), channel_id=1, replica_groups=mesh['grp'=4,'word'=8] {'grp'}, use_global_device_ids=true, to_apply=%region_6.7 | all-reduce | flops 1024 | bytes 8192 | tf_op jit(solution)/shard_map/psum | solution.py:7
  116.4 2.7 %multiply_reduce_fusion.1 = f32[8192]{0:T(1024)S(1)} fusion(bf16[8192,128]{1,0:T(8,128)(2,1)} %bitcast.12), kind=kLoop, calls=%fused_computation.13 | loop fusion | flops 3137536 | bytes 2129920 | tf_op jit(solution)/shard_map/reduce_sum | solution.py:35
  119.1 21.1 %all-reduce.5.cloned.1.call-done = f32[1024,128]{1,0:T(8,128)} async-done(((f32[1024,128]{1,0:T(8,128)}), f32[1024,128]{1,0:T(8,128)}) %all-reduce.5.cloned.1.call-update) | async-done | bytes 524304 | tf_op jit(solution)/shard_map/psum | solution.py:7
  140.2 1.4 multiply_reduce_fusion.2
  141.6 0.6 constant_dynamic-slice_fusion.1
  142.2 7.3 %multiply_reduce_fusion = f32[8192]{0:T(1024)} fusion(f32[1024]{0:T(1024)S(1)} %get-tuple-element.67, f32[8192]{0:T(1024)S(1)} %multiply_reduce_fusion.1, bf16[1024,128]{1,0:T(8,128)(2,1)S(1)} %get-tuple-element.68, bf16[8192,128]{1,0:T(8,128)(2,1)S(1)} %bitcast.13), kind=kOutput, calls=%fused_computation.12 | convolution fusion | flops 2189418496 | bytes 2428928 | tf_op jit(solution)/shard_map/dot_general | solution.py:42
  (20 shorter events, 0.1 us)
Async XLA Ops:
  7.2 85.6 %all-reduce.3.cloned.1.call-start = ((), (), s32[]{:S(2)}) async-start(), calls=%async_computation | async-start | bytes 1048576 | tf_op jit(solution)/shard_map/psum | solution.py:7
  32.5 0.8 copy-start.1
  32.5 109.7 %copy-start = (bf16[8,1024,128]{2,1,0:T(8,128)(2,1)S(1)}, bf16[8,1024,128]{2,1,0:T(8,128)(2,1)}, u32[]{:S(2)}) copy-start(bf16[8,1024,128]{2,1,0:T(8,128)(2,1)} %get-tuple-element.123) | copy-start | bytes 6291460
  33.3 106.8 %all-reduce.5.cloned.1.call-start = ((), (), s32[]{:S(2)}) async-start(), calls=%async_computation.1 | async-start | bytes 1048576 | tf_op jit(solution)/shard_map/psum | solution.py:7
Sparse Core Ops, SparseCore 0:
  33.5 59.2 all-reduce.2
  95.7 44.4 all-reduce.4
